TPU v7x, 512 devices: a whole 4x4x16 slice. The times are simulated.
512 devices in a mesh: row: 32 (over z, core), col: 16 (over x, y).
Axes of the slice: x: 4, y: 4, z: 16, core: 2. Of those that a mesh axis runs over, the one named last changes fastest.
Arguments:
- front_entries: float32 [16384, 16384], P('row', 'col'), may hold values from 0 to 3, as said below
- tile_group: int32 [32], replicated, may hold values from 0 to 3
- child_factor: bfloat16 [16384, 256], P('row', 'col'), may hold values from -0.375 to 0.375
- row_map: int32 [128], replicated, may hold values from 0 to 127, as said below
Outputs:
- factor_panels: bfloat16 [16384, 512], P('row', 'col')
- schur_block: float32 [16384, 16384], P('row', 'col')
Inputs may be any that keep to these rules, and one draw needn't show every extreme that they name: `front_entries`: Symmetric; assembled is positive definite. `row_map`: A permutation of the parent tiles. The tile in row block r (blocks of 512 rows) goes to a parent tile in row block r or in the row block whose index differs from r in the highest bit.
All inputs are finite; a program needn't handle non-finite values.
Results may differ from a plain program's by a relative error of at most 0.0026.
Values may be sent and summed in bfloat16 or wider, within the bound.
A program may use at most 64 MiB of HBM per device.

v0:
```python
import jax
import jax.numpy as jnp
from jax import lax
from jax.sharding import PartitionSpec as P

PW = 256
NP = 2
TS = 128
MT = 512


def swapped(value, axis, stride):
    mask = 2**stride
    pairs = [(source, source ^ mask) for source in range(lax.axis_size(axis))]
    return lax.ppermute(value, axis, pairs)


def broadcast(value, axis, source):
    kept = jnp.where(lax.axis_index(axis) == source, value, 0).astype(value.dtype)
    return lax.psum(kept, axis)


def panel_columns(matrix, offset, width_cols, fan_ratio, block_rows):
    return jnp.concatenate(
        [
            matrix[:, q * block_rows + offset : q * block_rows + offset + width_cols]
            for q in range(fan_ratio)
        ],
        axis=1,
    )


def outer_rows(left, right):
    return jnp.einsum("ik,jk->ij", left, right, preferred_element_type=jnp.float32)


def subtract_block(matrix, lead_rows, owner, low, col_from, col_to, base_col):
    region = matrix[low:, base_col + col_from : base_col + col_to]
    return matrix.at[low:, base_col + col_from : base_col + col_to].set(
        region - outer_rows(lead_rows, owner[col_from:col_to])
    )


def right_solve(lower_factor, strip):
    return lax.linalg.triangular_solve(
        lower_factor, strip, left_side=False, lower=True, transpose_a=True
    )


def local(front_entries, tile_group, child_factor, row_map):
    row_count = lax.axis_size("row")
    col_count = lax.axis_size("col")
    fan_ratio = row_count // col_count
    local_rows = front_entries.shape[0]
    local_cols = front_entries.shape[1]
    my_row = lax.axis_index("row")
    my_col = lax.axis_index("col")
    row_tiles = local_rows // MT
    col_tiles = local_cols // MT
    group_rows = lax.dynamic_slice_in_dim(tile_group, my_row * row_tiles, row_tiles)
    group_cols = lax.dynamic_slice_in_dim(tile_group, my_col * col_tiles, col_tiles)
    same_group = (group_rows[:, None] == group_cols[None, :]).astype(jnp.float32)
    masked = (
        front_entries.reshape(row_tiles, MT, col_tiles, MT) * same_group[:, None, :, None]
    ).reshape(local_rows, local_cols)
    child_full = lax.all_gather(child_factor, "col", axis=1, tiled=True)
    child_width = child_full.shape[1]
    partner_full = swapped(child_full, "row", row_count.bit_length() - 2)
    tile_count = local_rows // TS
    partner_row = jnp.bitwise_xor(my_row, row_count // 2)
    own_map = lax.dynamic_slice_in_dim(row_map, my_row * tile_count, tile_count)
    partner_map = lax.dynamic_slice_in_dim(row_map, partner_row * tile_count, tile_count)
    slot_ids = my_row * tile_count + jnp.arange(tile_count, dtype=jnp.int32)

    def place_tiles(tile_map, source):
        chooser = (tile_map[None, :] == slot_ids[:, None]).astype(jnp.bfloat16)
        placed = jnp.dot(
            chooser,
            source.reshape(tile_count, TS * child_width),
            preferred_element_type=jnp.float32,
        )
        return placed.astype(jnp.bfloat16).reshape(local_rows, child_width)

    own_parent = place_tiles(own_map, child_full)
    partner_parent = place_tiles(partner_map, partner_full)
    lower_half = my_row < row_count // 2
    child_wide = jnp.where(
        lower_half,
        jnp.concatenate([own_parent, partner_parent], axis=1),
        jnp.concatenate([partner_parent, own_parent], axis=1),
    )
    child_owners = [broadcast(child_wide, "row", fan_ratio * my_col + q) for q in range(fan_ratio)]
    matrix = jnp.concatenate(
        [
            masked[:, q * local_rows : (q + 1) * local_rows]
            + outer_rows(child_wide, child_owners[q])
            for q in range(fan_ratio)
        ],
        axis=1,
    )
    row_share = PW // row_count
    col_share = PW // col_count
    local_ids = jnp.arange(local_rows)
    coming = None
    outputs = []
    for k in range(NP):
        offset = k * row_share
        panel_strip = panel_columns(matrix, offset, row_share, fan_ratio, local_rows)
        corner = panel_strip[offset : offset + row_share]
        gathered = lax.all_gather(corner, ("row", "col"), axis=0, tiled=True)
        diagonal = (
            gathered.reshape(row_count, col_count, row_share, col_share)
            .transpose(0, 2, 1, 3)
            .reshape(PW, PW)
        )
        lower_factor = jnp.linalg.cholesky(diagonal)
        whole_strip = lax.all_gather(panel_strip, "col", axis=1, tiled=True)
        rounded = right_solve(lower_factor, whole_strip).astype(jnp.bfloat16)
        own_lower = lax.dynamic_slice_in_dim(lower_factor, my_row * row_share, row_share).astype(
            jnp.bfloat16
        )
        rounded = jnp.where((local_ids < offset)[:, None], jnp.zeros_like(rounded), rounded)
        rounded = rounded.at[offset : offset + row_share].set(own_lower)
        outputs.append(lax.dynamic_slice_in_dim(rounded, my_col * col_share, col_share, 1))
        owners = [broadcast(rounded, "row", fan_ratio * my_col + q) for q in range(fan_ratio)]
        low = offset + row_share
        lead_rows = rounded[low:]
        for q in range(fan_ratio):
            matrix = subtract_block(
                matrix, lead_rows, owners[q], low, low, local_rows, q * local_rows
            )
    pivot_done = NP * row_share
    row_keep = local_ids >= pivot_done
    col_keep = jnp.arange(local_cols) % local_rows >= pivot_done
    schur_block = jnp.where(row_keep[:, None] & col_keep[None, :], matrix, jnp.zeros_like(matrix))
    factor_panels = jnp.concatenate(outputs, axis=1)
    return (factor_panels, schur_block)


def solution(mesh):
    placed = (P("row", "col"), P(), P("row", "col"), P())
    return jax.shard_map(
        local,
        mesh=mesh,
        in_specs=placed,
        out_specs=(P("row", "col"), P("row", "col")),
        check_vma=False,
    )
```

profile of v0, /device:TPU:1, one launch (start us, length us, event | category | flops | bytes accessed | tf_op | source)
XLA Modules:
  0.0 1302.7 jit_solution(17513636110733798873)
XLA Ops:
  7.2 19.7 %all_gather.15 = bf16[512,256]{0,1:T(8,128)(2,1)S(1)} all-gather(bf16[512,16]{0,1:T(8,128)(2,1)} %param.21), channel_id=1, replica_groups=mesh['row'=32,'col'=16] {'col'}, dimensions={1}, use_global_device_ids=true | all-gather | bytes 278528 | tf_op jit(solution)/shard_map/all_gather | solution.py:66
  26.9 15.4 %collective-permute-start = (bf16[512,256]{0,1:T(8,128)(2,1)S(1)}, bf16[512,256]{0,1:T(8,128)(2,1)S(1)}, u32[]{:S(2)}, u32[]{:S(2)}) collective-permute-start(bf16[512,256]{0,1:T(8,128)(2,1)S(1)} %all_gather.15), channel_id=1, source_target_pairs={{0,256},{16,272},{32,288},{48,304},{64,320},{80,336},{96,352},{112... | collective-permute-start | bytes 786440 | tf_op jit(solution)/shard_map/ppermute | solution.py:15
  51.2 226.5 %all-reduce.12.cloned.1.call-done = (bf16[512,512]{1,0:T(8,128)(2,1)}, bf16[512,512]{1,0:T(8,128)(2,1)}) async-done(((bf16[512,512]{1,0:T(8,128)(2,1)}, bf16[512,512]{1,0:T(8,128)(2,1)}), (bf16[512,512]{1,0:T(8,128)(2,1)}, bf16[512,512]{1,0:T(8,128)(2,1)})) %all-reduce.12.cloned.1.call-update) | async-done | bytes 1048592 | tf_op jit(solution)/shard_map/psum | solution.py:20
  281.4 198.2 %all_gather.16 = f32[4096,16]{1,0:T(8,128)S(1)} all-gather(f32[8,16]{1,0:T(8,128)S(1)} %copy.33), channel_id=1, replica_groups=mesh['row'=32,'col'=16] {'row','col'}, dimensions={0}, use_global_device_ids=true | all-gather | bytes 262656 | tf_op jit(solution)/shard_map/all_gather | solution.py:110
  481.1 11.7 cholesky.130
  492.8 9.8 custom-call.13
  503.1 11.9 cholesky.147
  517.6 3.8 while.10
  521.5 19.7 %custom-call.14 = f32[2,128,128]{1,2,0:T(8,128)S(1)} custom-call(f32[2,128,128]{2,1,0:T(8,128)S(1)} %get-tuple-element.90), custom_call_target="InvertDiagBlocksLowerTriangular" | custom-call | tf_op jit(solution)/shard_map/triangular_solve/custom-call.0 | solution.py:45
  541.2 16.2 %all_gather.17 = f32[512,256]{0,1:T(8,128)S(1)} all-gather(f32[512,16]{0,1:T(8,128)S(1)} %pad_maximum_fusion.1), channel_id=1, replica_groups=mesh['row'=32,'col'=16] {'col'}, dimensions={1}, use_global_device_ids=true | all-gather | bytes 557056 | tf_op jit(solution)/shard_map/all_gather | solution.py:117
  561.5 209.2 %all-reduce.10.cloned.1.call-done = (bf16[512,256]{0,1:T(8,128)(2,1)}, bf16[512,256]{0,1:T(8,128)(2,1)}) async-done(((bf16[512,256]{0,1:T(8,128)(2,1)}, bf16[512,256]{0,1:T(8,128)(2,1)}), (bf16[512,256]{0,1:T(8,128)(2,1)}, bf16[512,256]{0,1:T(8,128)(2,1)})) %all-reduce.10.cloned.1.call-update) | async-done | bytes 524304 | tf_op jit(solution)/shard_map/psum | solution.py:20
  773.2 5.4 scatter.21
  780.2 3.4 scatter.24
  783.8 197.6 %all_gather.18 = f32[4096,16]{1,0:T(8,128)S(1)} all-gather(f32[8,16]{1,0:T(8,128)S(1)} %copy.38), channel_id=1, replica_groups=mesh['row'=32,'col'=16] {'row','col'}, dimensions={0}, use_global_device_ids=true | all-gather | bytes 262656 | tf_op jit(solution)/shard_map/all_gather | solution.py:110
  986.0 11.7 cholesky.164
  997.8 9.8 custom-call.15
  1008.1 11.7 cholesky.181
  1022.4 4.0 while.11
  1026.5 19.9 %custom-call.16 = f32[2,128,128]{1,2,0:T(8,128)S(1)} custom-call(f32[2,128,128]{2,1,0:T(8,128)S(1)} %get-tuple-element.91), custom_call_target="InvertDiagBlocksLowerTriangular" | custom-call | tf_op jit(solution)/shard_map/triangular_solve/custom-call.0 | solution.py:45
  1046.4 16.3 %all_gather.19 = f32[512,256]{0,1:T(8,128)S(1)} all-gather(f32[512,16]{0,1:T(8,128)S(1)} %pad_maximum_fusion.2), channel_id=1, replica_groups=mesh['row'=32,'col'=16] {'col'}, dimensions={1}, use_global_device_ids=true | all-gather | bytes 557056 | tf_op jit(solution)/shard_map/all_gather | solution.py:117
  1066.2 210.0 %all-reduce.8.cloned.1.call-done = (bf16[512,256]{0,1:T(8,128)(2,1)}, bf16[512,256]{0,1:T(8,128)(2,1)}) async-done(((bf16[512,256]{0,1:T(8,128)(2,1)}, bf16[512,256]{0,1:T(8,128)(2,1)}), (bf16[512,256]{0,1:T(8,128)(2,1)}, bf16[512,256]{0,1:T(8,128)(2,1)})) %all-reduce.8.cloned.1.call-update) | async-done | bytes 524304 | tf_op jit(solution)/shard_map/psum | solution.py:20
  1278.8 5.4 scatter.26
  1285.8 5.6 scatter.29
  1293.0 2.9 copy.45
  (118 shorter events, 47.5 us)
Async XLA Ops:
  7.2 36.9 %copy-start.5 = (s32[32]{0:T(128)S(1)}, s32[32]{0:T(128)}, u32[]{:S(2)}) copy-start(s32[32]{0:T(128)} %param.20) | copy-start | bytes 388
  7.2 270.5 %all-reduce.12.cloned.1.call-start = ((), (), s32[]{:S(2)}) async-start(), calls=%async_computation.2 | async-start | bytes 2097152 | tf_op jit(solution)/shard_map/psum | solution.py:20
  26.9 20.5 %collective-permute-start = (bf16[512,256]{0,1:T(8,128)(2,1)S(1)}, bf16[512,256]{0,1:T(8,128)(2,1)S(1)}, u32[]{:S(2)}, u32[]{:S(2)}) collective-permute-start(bf16[512,256]{0,1:T(8,128)(2,1)S(1)} %all_gather.15), channel_id=1, source_target_pairs={{0,256},{16,272},{32,288},{48,304},{64,320},{80,336},{96,352},{112... | collective-permute-start | bytes 786440 | tf_op jit(solution)/shard_map/ppermute | solution.py:15
  48.3 2.9 copy-start.2
  49.6 721.1 %all-reduce.10.cloned.1.call-start = ((), (), s32[]{:S(2)}) async-start(), calls=%async_computation.1 | async-start | bytes 1048576 | tf_op jit(solution)/shard_map/psum | solution.py:20
  51.2 228.6 %copy-start = (f32[512,1024]{0,1:T(8,128)S(1)}, f32[512,1024]{0,1:T(8,128)}, u32[]{:S(2)}) copy-start(f32[512,1024]{0,1:T(8,128)} %broadcast_multiply_fusion) | copy-start | bytes 6291460
  277.7 2.1 copy-start.3
  277.7 2.1 copy-start.6
  280.3 1.0 copy-start.1
  560.0 716.2 %all-reduce.8.cloned.1.call-start = ((), (), s32[]{:S(2)}) async-start(), calls=%async_computation | async-start | bytes 1048576 | tf_op jit(solution)/shard_map/psum | solution.py:20
  1276.2 8.0 copy-start.4
Sparse Core Ops, SparseCore 0:
  49.7 227.9 all-reduce.11
  560.1 210.4 all-reduce.9
  1065.7 210.4 all-reduce.7
where the time goes:
time: 1310 us; the launch traced here: 1300 us
  waiting for transfers between devices  646 us (49%)
  blocking collectives  448 us (34%)
  other arithmetic  119 us (9%)
  local copies, waits for them, and re-layouts  42.4 us (3%)
  between operations  17.1 us (1%)
  starting transfers between devices  15.5 us (1%)
  matrix products  15 us (1%)
    psum x3, waiting for transfers between devices, broadcast(): return lax.psum(kept, axis)  646 us
    all_gather x2, blocking collectives, local(): gathered = lax.all_gather(corner, ('row', 'col'), axis=0, tiled=True)  396 us
    another operation x14, other arithmetic, local(): lower_factor = jnp.linalg.cholesky(diagonal)  69.3 us
    another operation x5, other arithmetic, right_solve(): lax.linalg.triangular_solve(lower_factor, strip, left_side=False, lower=T...  39.7 us
    all_gather x2, blocking collectives, local(): whole_strip = lax.all_gather(panel_strip, 'col', axis=1, tiled=True)  32.5 us
  transfers between devices with their start and end apart: 4, of which 3 were waited for; matrix products, arithmetic and copies ran while one was open for 1% of the time, Pallas kernels for 0%

commit v1 on v0

--- a/solution.py
+++ b/solution.py
@@ -7,6 +7,19 @@
 NP = 2
 TS = 128
 MT = 512
+
+
+def ring_gather(x, axis, dim):
+    ways = lax.axis_size(axis)
+    up = [(d, (d + 1) % ways) for d in range(ways)]
+    down = [(d, (d - 1) % ways) for d in range(ways)]
+    earlier, later = ([x], [x])
+    for _ in range(ways // 2):
+        earlier.append(lax.ppermute(earlier[-1], axis, up))
+    for _ in range((ways - 1) // 2):
+        later.append(lax.ppermute(later[-1], axis, down))
+    line = jnp.concatenate([*earlier[::-1], *later[1:]], axis=dim)
+    return jnp.roll(line, (lax.axis_index(axis) - ways // 2) * x.shape[dim], axis=dim)
 
 
 def swapped(value, axis, stride):
@@ -114,7 +127,7 @@
             .reshape(PW, PW)
         )
         lower_factor = jnp.linalg.cholesky(diagonal)
-        whole_strip = lax.all_gather(panel_strip, "col", axis=1, tiled=True)
+        whole_strip = ring_gather(panel_strip, "col", 1)
         rounded = right_solve(lower_factor, whole_strip).astype(jnp.bfloat16)
         own_lower = lax.dynamic_slice_in_dim(lower_factor, my_row * row_share, row_share).astype(
             jnp.bfloat16

time: 1310 us -> 1400 us (1.069)
  starting transfers between devices: 15.5 us -> 142 us
  blocking collectives: 448 us -> 409 us
    ppermute x0 -> x30, starting transfers between devices: none -> 127 us  [the longest x14 91.1 us: ring_gather(): later.append(lax.ppermute(later[-1], axis, down))]
    all_gather x2 -> x0, blocking collectives: 32.5 us -> none  [local(): whole_strip = lax.all_gather(panel_strip, 'col', axis=1, tiled=True)]
  transfers between devices with their start and end apart: 4 -> 34, of which waited for: 3 -> 5; matrix products, arithmetic and copies ran while one was open for 1% -> 10% of each run, Pallas kernels for 0% -> 0%
where the time goes in v1:
time: 1400 us
  waiting for transfers between devices  651 us (46%)
  blocking collectives  409 us (29%)
  starting transfers between devices  142 us (10%)
  other arithmetic  119 us (8%)
  local copies, waits for them, and re-layouts  43.3 us (3%)
  between operations  17.8 us (1%)
  matrix products  15 us (1%)
    psum x3, waiting for transfers between devices, broadcast(): return lax.psum(kept, axis)  650 us
    all_gather x2, blocking collectives, local(): gathered = lax.all_gather(corner, ('row', 'col'), axis=0, tiled=True)  389 us
    ppermute x14, starting transfers between devices, ring_gather(): later.append(lax.ppermute(later[-1], axis, down))  91.1 us
    another operation x14, other arithmetic, local(): lower_factor = jnp.linalg.cholesky(diagonal)  69.2 us
    another operation x5, other arithmetic, right_solve(): lax.linalg.triangular_solve(lower_factor, strip, left_side=False, lower=T...  39.4 us
    ppermute x16, starting transfers between devices, ring_gather(): earlier.append(lax.ppermute(earlier[-1], axis, up))  35.6 us
  transfers between devices with their start and end apart: 34, of which 5 were waited for; matrix products, arithmetic and copies ran while one was open for 10% of the time, Pallas kernels for 0%

profile of v1, /device:TPU:1, one launch (start us, length us, event | category | flops | bytes accessed | tf_op | source)
XLA Modules:
  0.0 1397.0 jit_solution(11472560034165706275)
XLA Ops:
  7.2 19.7 %all_gather.9 = bf16[512,256]{0,1:T(8,128)(2,1)S(1)} all-gather(bf16[512,16]{0,1:T(8,128)(2,1)} %param.23), channel_id=1, replica_groups=mesh['row'=32,'col'=16] {'col'}, dimensions={1}, use_global_device_ids=true | all-gather | bytes 278528 | tf_op jit(solution)/shard_map/all_gather | solution.py:79
  26.9 15.4 %collective-permute-start = (bf16[512,256]{0,1:T(8,128)(2,1)S(1)}, bf16[512,256]{0,1:T(8,128)(2,1)S(1)}, u32[]{:S(2)}, u32[]{:S(2)}) collective-permute-start(bf16[512,256]{0,1:T(8,128)(2,1)S(1)} %all_gather.9), channel_id=1, source_target_pairs={{0,256},{16,272},{32,288},{48,304},{64,320},{80,336},{96,352},{112... | collective-permute-start | bytes 786440 | tf_op jit(solution)/shard_map/ppermute | solution.py:28
  51.1 226.5 %all-reduce.12.cloned.1.call-done = (bf16[512,512]{1,0:T(8,128)(2,1)}, bf16[512,512]{1,0:T(8,128)(2,1)}) async-done(((bf16[512,512]{1,0:T(8,128)(2,1)}, bf16[512,512]{1,0:T(8,128)(2,1)}), (bf16[512,512]{1,0:T(8,128)(2,1)}, bf16[512,512]{1,0:T(8,128)(2,1)})) %all-reduce.12.cloned.1.call-update) | async-done | bytes 1048592 | tf_op jit(solution)/shard_map/psum | solution.py:33
  289.9 194.6 %all_gather.10 = f32[4096,16]{1,0:T(8,128)S(1)} all-gather(f32[8,16]{1,0:T(8,128)S(1)} %copy.33), channel_id=1, replica_groups=mesh['row'=32,'col'=16] {'row','col'}, dimensions={0}, use_global_device_ids=true | all-gather | bytes 262656 | tf_op jit(solution)/shard_map/all_gather | solution.py:123
  486.0 11.7 cholesky.130
  497.7 9.8 custom-call.13
  511.3 11.7 cholesky.147
  544.9 6.7 collective-permute-start.12
  553.6 6.7 collective-permute-start.13
  566.4 6.7 collective-permute-start.14
  575.0 19.7 %custom-call.14 = f32[2,128,128]{1,2,0:T(8,128)S(1)} custom-call(f32[2,128,128]{2,1,0:T(8,128)S(1)} %get-tuple-element.91), custom_call_target="InvertDiagBlocksLowerTriangular" | custom-call | tf_op jit(solution)/shard_map/triangular_solve/custom-call.0 | solution.py:58
  594.8 6.7 collective-permute-start.15
  606.6 211.2 %all-reduce.10.cloned.1.call-done = (bf16[512,256]{0,1:T(8,128)(2,1)}, bf16[512,256]{0,1:T(8,128)(2,1)}) async-done(((bf16[512,256]{0,1:T(8,128)(2,1)}, bf16[512,256]{0,1:T(8,128)(2,1)}), (bf16[512,256]{0,1:T(8,128)(2,1)}, bf16[512,256]{0,1:T(8,128)(2,1)})) %all-reduce.10.cloned.1.call-update) | async-done | bytes 524304 | tf_op jit(solution)/shard_map/psum | solution.py:33
  839.6 194.8 %all_gather.11 = f32[4096,16]{1,0:T(8,128)S(1)} all-gather(f32[8,16]{1,0:T(8,128)S(1)} %copy.38), channel_id=1, replica_groups=mesh['row'=32,'col'=16] {'row','col'}, dimensions={0}, use_global_device_ids=true | all-gather | bytes 262656 | tf_op jit(solution)/shard_map/all_gather | solution.py:123
  1038.7 11.7 cholesky.164
  1050.5 9.8 custom-call.15
  1063.9 11.7 cholesky.181
  1077.6 6.7 collective-permute-start.25
  1097.4 6.7 collective-permute-start.27
  1106.1 6.7 collective-permute-start.28
  1118.8 6.7 collective-permute-start.29
  1127.4 19.7 %custom-call.16 = f32[2,128,128]{1,2,0:T(8,128)S(1)} custom-call(f32[2,128,128]{2,1,0:T(8,128)S(1)} %get-tuple-element.92), custom_call_target="InvertDiagBlocksLowerTriangular" | custom-call | tf_op jit(solution)/shard_map/triangular_solve/custom-call.0 | solution.py:58
  1147.2 6.7 collective-permute-start.30
  1158.5 212.0 %all-reduce.8.cloned.1.call-done = (bf16[512,256]{0,1:T(8,128)(2,1)}, bf16[512,256]{0,1:T(8,128)(2,1)}) async-done(((bf16[512,256]{0,1:T(8,128)(2,1)}, bf16[512,256]{0,1:T(8,128)(2,1)}), (bf16[512,256]{0,1:T(8,128)(2,1)}, bf16[512,256]{0,1:T(8,128)(2,1)})) %all-reduce.8.cloned.1.call-update) | async-done | bytes 524304 | tf_op jit(solution)/shard_map/psum | solution.py:33
  (212 shorter events, 147.0 us)
Async XLA Ops:
  7.2 270.4 %all-reduce.12.cloned.1.call-start = ((), (), s32[]{:S(2)}) async-start(), calls=%async_computation.2 | async-start | bytes 2097152 | tf_op jit(solution)/shard_map/psum | solution.py:33
  26.9 20.5 %collective-permute-start = (bf16[512,256]{0,1:T(8,128)(2,1)S(1)}, bf16[512,256]{0,1:T(8,128)(2,1)S(1)}, u32[]{:S(2)}, u32[]{:S(2)}) collective-permute-start(bf16[512,256]{0,1:T(8,128)(2,1)S(1)} %all_gather.9), channel_id=1, source_target_pairs={{0,256},{16,272},{32,288},{48,304},{64,320},{80,336},{96,352},{112... | collective-permute-start | bytes 786440 | tf_op jit(solution)/shard_map/ppermute | solution.py:28
  49.5 768.3 %all-reduce.10.cloned.1.call-start = ((), (), s32[]{:S(2)}) async-start(), calls=%async_computation.1 | async-start | bytes 1048576 | tf_op jit(solution)/shard_map/psum | solution.py:33
  281.2 226.6 %collective-permute-start.1 = (f32[512,16]{0,1:T(8,128)S(1)}, f32[512,16]{0,1:T(8,128)S(1)}, u32[]{:S(2)}, u32[]{:S(2)}) collective-permute-start(f32[512,16]{0,1:T(8,128)S(1)} %pad_maximum_fusion.1), channel_id=1, source_target_pairs={{0,1},{1,2},{2,3},{3,4},{4,5},{5,6},{6,7},{7,8},{8,9},{9,10},{10,1... | collective-permute-start | bytes 98312 | tf_op jit(solution)/shard_map/ppermute | solution.py:18
  284.3 240.6 %collective-permute-start.9 = (f32[512,16]{0,1:T(8,128)S(1)}, f32[512,16]{0,1:T(8,128)S(1)}, u32[]{:S(2)}, u32[]{:S(2)}) collective-permute-start(f32[512,16]{0,1:T(8,128)S(1)} %pad_maximum_fusion.1), channel_id=1, source_target_pairs={{0,15},{1,0},{2,1},{3,2},{4,3},{5,4},{6,5},{7,6},{8,7},{9,8},{10,9... | collective-permute-start | bytes 98312 | tf_op jit(solution)/shard_map/ppermute | solution.py:20
  507.8 15.2 %collective-permute-start.2 = (f32[512,16]{0,1:T(8,128)S(1)}, f32[512,16]{0,1:T(8,128)S(1)}, u32[]{:S(2)}, u32[]{:S(2)}) collective-permute-start(f32[512,16]{0,1:T(8,128)S(1)} %collective-permute-done.1), channel_id=1, source_target_pairs={{0,1},{1,2},{2,3},{3,4},{4,5},{5,6},{6,7},{7,8},{8,9},{9,10},{10,1... | collective-permute-start | bytes 98312 | tf_op jit(solution)/shard_map/ppermute | solution.py:18
  525.0 9.3 collective-permute-start.10
  531.7 9.3 collective-permute-start.4
  534.3 10.6 collective-permute-start.11
  541.0 10.6 collective-permute-start.5
  553.6 12.8 collective-permute-start.13
  560.3 12.8 collective-permute-start.7
  566.4 28.5 %collective-permute-start.14 = (f32[512,16]{0,1:T(8,128)S(1)}, f32[512,16]{0,1:T(8,128)S(1)}, u32[]{:S(2)}, u32[]{:S(2)}) collective-permute-start(f32[512,16]{0,1:T(8,128)S(1)} %collective-permute-done.13), channel_id=1, source_target_pairs={{0,15},{1,0},{2,1},{3,2},{4,3},{5,4},{6,5},{7,6},{8,7},{9,8},{10,9... | collective-permute-start | bytes 98312 | tf_op jit(solution)/shard_map/ppermute | solution.py:20
  573.1 28.5 %collective-permute-start.8 = (f32[512,16]{0,1:T(8,128)S(1)}, f32[512,16]{0,1:T(8,128)S(1)}, u32[]{:S(2)}, u32[]{:S(2)}) collective-permute-start(f32[512,16]{0,1:T(8,128)S(1)} %collective-permute-done.7), channel_id=1, source_target_pairs={{0,1},{1,2},{2,3},{3,4},{4,5},{5,6},{6,7},{7,8},{8,9},{9,10},{10,1... | collective-permute-start | bytes 98312 | tf_op jit(solution)/shard_map/ppermute | solution.py:18
  605.1 765.4 %all-reduce.8.cloned.1.call-start = ((), (), s32[]{:S(2)}) async-start(), calls=%async_computation | async-start | bytes 1048576 | tf_op jit(solution)/shard_map/psum | solution.py:33
  830.9 229.6 %collective-permute-start.16 = (f32[512,16]{0,1:T(8,128)S(1)}, f32[512,16]{0,1:T(8,128)S(1)}, u32[]{:S(2)}, u32[]{:S(2)}) collective-permute-start(f32[512,16]{0,1:T(8,128)S(1)} %pad_maximum_fusion.2), channel_id=1, source_target_pairs={{0,1},{1,2},{2,3},{3,4},{4,5},{5,6},{6,7},{7,8},{8,9},{9,10},{10,1... | collective-permute-start | bytes 98312 | tf_op jit(solution)/shard_map/ppermute | solution.py:18
  834.0 243.6 %collective-permute-start.24 = (f32[512,16]{0,1:T(8,128)S(1)}, f32[512,16]{0,1:T(8,128)S(1)}, u32[]{:S(2)}, u32[]{:S(2)}) collective-permute-start(f32[512,16]{0,1:T(8,128)S(1)} %pad_maximum_fusion.2), channel_id=1, source_target_pairs={{0,15},{1,0},{2,1},{3,2},{4,3},{5,4},{6,5},{7,6},{8,7},{9,8},{10,9... | collective-permute-start | bytes 98312 | tf_op jit(solution)/shard_map/ppermute | solution.py:20
  1060.5 15.1 %collective-permute-start.17 = (f32[512,16]{0,1:T(8,128)S(1)}, f32[512,16]{0,1:T(8,128)S(1)}, u32[]{:S(2)}, u32[]{:S(2)}) collective-permute-start(f32[512,16]{0,1:T(8,128)S(1)} %collective-permute-done.16), channel_id=1, source_target_pairs={{0,1},{1,2},{2,3},{3,4},{4,5},{5,6},{6,7},{7,8},{8,9},{9,10},{10,1... | collective-permute-start | bytes 98312 | tf_op jit(solution)/shard_map/ppermute | solution.py:18
  1086.9 10.6 collective-permute-start.26
  1093.6 10.6 collective-permute-start.20
  1106.1 12.7 collective-permute-start.28
  1112.8 12.7 collective-permute-start.22
  1118.8 28.5 %collective-permute-start.29 = (f32[512,16]{0,1:T(8,128)S(1)}, f32[512,16]{0,1:T(8,128)S(1)}, u32[]{:S(2)}, u32[]{:S(2)}) collective-permute-start(f32[512,16]{0,1:T(8,128)S(1)} %collective-permute-done.28), channel_id=1, source_target_pairs={{0,15},{1,0},{2,1},{3,2},{4,3},{5,4},{6,5},{7,6},{8,7},{9,8},{10,9... | collective-permute-start | bytes 98312 | tf_op jit(solution)/shard_map/ppermute | solution.py:20
  1125.5 28.5 %collective-permute-start.23 = (f32[512,16]{0,1:T(8,128)S(1)}, f32[512,16]{0,1:T(8,128)S(1)}, u32[]{:S(2)}, u32[]{:S(2)}) collective-permute-start(f32[512,16]{0,1:T(8,128)S(1)} %collective-permute-done.22), channel_id=1, source_target_pairs={{0,1},{1,2},{2,3},{3,4},{4,5},{5,6},{6,7},{7,8},{8,9},{9,10},{10,1... | collective-permute-start | bytes 98312 | tf_op jit(solution)/shard_map/ppermute | solution.py:18
  (17 other events, 367.5 us)
Sparse Core Ops, SparseCore 0:
  49.6 227.9 all-reduce.11
  605.2 212.4 all-reduce.9
  1157.9 212.5 all-reduce.7
